TPU v7x, 128 devices: a whole 4x4x4 slice. The times are simulated.
128 devices in a mesh: trace: 8 (over y, core), gx: 4 (over z), gy: 4 (over x).
Axes of the slice: x: 4, y: 4, z: 4, core: 2. Of those that a mesh axis runs over, the one named last changes fastest.
Arguments:
- traces: bfloat16 [32768, 4, 256], P(('trace', 'gx', 'gy')), may hold values from -4 to 4
- coupling: bfloat16 [32768, 4], P(('trace', 'gx', 'gy')), may hold values from 0.099609375 to 1.8984375
- tap_shift: int32 [32768], P(('trace', 'gx', 'gy')), may hold values from 0 to 63
- node_tile: int32 [32768, 1], P(('trace', 'gx', 'gy')), may hold values from 0 to 127; in each aligned block of 256 rows (0 to 255, 256 to 511, ...) at most 4 rows name the same one
- node_cell: int32 [32768], P(('trace', 'gx', 'gy')), may hold values from 0 to 524287
- field_prev: float32 [64, 1024, 1024], P('trace', 'gx', 'gy'), may hold values from -0.3125 to 0.3125
- field_now: float32 [64, 1024, 1024], P('trace', 'gx', 'gy'), may hold values from -0.3125 to 0.3125
- speed_sq: float32 [64, 1024, 1024], P('trace', 'gx', 'gy'), may hold values from 0.3 to 1
Outputs:
- out_prev: float32 [64, 1024, 1024], P('trace', 'gx', 'gy')
- out_now: float32 [64, 1024, 1024], P('trace', 'gx', 'gy')
Inputs may be any that keep to these rules, and one draw needn't show every extreme that they name: `node_tile`: among the nodes of one device at most 4 lie in one tile, and some device has exactly 4 in some tile.
All inputs are finite; a program needn't handle non-finite values.
Results may differ from a plain program's by a relative error of at most 0.0003.
Values may be sent and summed in bfloat16 or wider, within the bound.
A program may use at most 128 MiB of HBM per device.

v0:
```python
import functools
import math

import jax
import jax.numpy as jnp
import numpy as np
from jax import lax
from jax.experimental import pallas as pl
from jax.experimental.pallas import tpu as pltpu
from jax.sharding import PartitionSpec as P

NT = 256
STEPS = 4
RATE = 64
CZ, CX, CY = 8, 256, 256
NT_AX, NGX, NGY = 8, 4, 4
CAP = 4
PAD = 8
ROWS = 32
MESH = pl.DeviceIdType.MESH
F32 = jnp.float32
BF16 = jnp.bfloat16


def window_table():
    u = (np.arange(NT)[None, :] + np.arange(NT)[:, None] - (NT - RATE // 2)).astype(np.float64)
    w = np.sinc(u / RATE) * 0.5 * (1.0 + np.cos(math.pi * u / (2.0 * RATE)))
    return np.where(np.abs(u) < 2.0 * RATE, w, 0.0).astype(np.float32)


def nt_dot(a, b, precision=None):
    return lax.dot_general(
        a, b, (((1,), (1,)), ((), ())), precision=precision, preferred_element_type=F32
    )


def kernel(
    comb_ref, win_ref, shift_ref, tile_ref, cell_ref, prev_hbm, now_hbm, speed_hbm,
    outp_hbm, outn_hbm,
    fa, fb, q, s_ref, gz, gx_buf, gy_buf, px, py, hy, rows_1h, v_hi, v_lo, t1, b1, b2, b3, b4,
    lsem, osem, zs, zr, xs, xr, ys, yr, a_s, a_r,
):
    t = lax.axis_index("trace")
    gx = lax.axis_index("gx")
    gy = lax.axis_index("gy")

    loads = [
        pltpu.make_async_copy(now_hbm, fa.at[:, pl.ds(PAD, CX), :], lsem.at[0]),
        pltpu.make_async_copy(prev_hbm, fb.at[:, pl.ds(PAD, CX), :], lsem.at[1]),
        pltpu.make_async_copy(speed_hbm, q, lsem.at[2]),
    ]
    for c in loads:
        c.start()

    sides = (("trace", t, NT_AX), ("gx", gx, NGX), ("gy", gy, NGY))
    for buf, (_, pos, count) in zip((gz, gx_buf, gy_buf), sides):
        for side in (0, 1):
            @pl.when(pos == (0 if side == 0 else count - 1))
            def _(buf=buf, side=side):
                for k in range(STEPS):
                    buf[k, side] = jnp.zeros(buf.shape[2:], F32)

    barrier = pltpu.get_barrier_semaphore()
    peers = []
    for axis, pos, count in sides:
        for d in range(1, count):
            peers.append((axis, lax.rem(pos + d, count)))
    for axis, j in peers:
        pl.semaphore_signal(barrier, inc=1, device_id={axis: j}, device_id_type=MESH)
    pl.semaphore_wait(barrier, len(peers))

    def halo(kind, k, d, src=None):
        axis, pos, count = sides[kind]
        ghost = (gz, gx_buf, gy_buf)[kind]
        ssem, rsem = ((zs, zr), (xs, xr), (ys, yr))[kind]
        if src is None:
            src = ghost.at[k, 1 - d]
        to = jnp.maximum(pos - 1, 0) if d == 0 else jnp.minimum(pos + 1, count - 1)
        return pltpu.make_async_remote_copy(
            src_ref=src,
            dst_ref=ghost.at[k, 1 - d],
            send_sem=ssem.at[k, d],
            recv_sem=rsem.at[k, 1 - d],
            device_id={axis: to},
            device_id_type=MESH,
        )

    def exists(kind, d):
        _, pos, count = sides[kind]
        return pos > 0 if d == 0 else pos < count - 1

    def send(kind, k, d, src):
        @pl.when(exists(kind, d))
        def _():
            halo(kind, k, d, src).start()

    def wait_ghost(kind, k):
        for side in (0, 1):
            @pl.when(exists(kind, side))
            def _(side=side):
                halo(kind, k, 1 - side).wait_recv()

    def wait_sent(kind, k):
        for d in (0, 1):
            @pl.when(exists(kind, d))
            def _(d=d):
                halo(kind, k, d).wait_send()

    send(0, 0, 0, now_hbm.at[0])
    send(0, 0, 1, now_hbm.at[CZ - 1])

    at = nt_dot(win_ref[...], comb_ref[...], lax.Precision.HIGHEST)
    shift = shift_ref[...]
    picked = lax.broadcasted_iota(jnp.int32, (RATE, NT), 0) == shift
    amps = [
        jnp.sum(jnp.where(picked, at[s * RATE:(s + 1) * RATE, :], 0.0), axis=0, keepdims=True)
        for s in range(STEPS)
    ]
    cell = cell_ref[...]
    cz = (cell // (CX * CY)).astype(F32)
    cx = ((cell // CY) % CX).astype(F32)
    cy = (cell % CY).astype(F32)
    hi = [a.astype(BF16).astype(F32) for a in amps]
    lo = [a - h for a, h in zip(amps, hi)]
    zero_row = jnp.zeros((1, NT), F32)
    vals = jnp.concatenate([cz, cx, cy] + hi + lo + [zero_row] * 5, axis=0).astype(BF16)
    tile = tile_ref[...]
    dest = (tile % NGY) * (NGX * NT_AX) + ((tile // NGY) % NGX) * NT_AX + tile // (NGX * NGY)
    n_dev = NT_AX * NGX * NGY
    onehot = lax.broadcasted_iota(jnp.int32, (n_dev, NT), 0) == dest
    onehot_f = jnp.where(onehot, 1.0, 0.0)
    before = jnp.where(
        lax.broadcasted_iota(jnp.int32, (NT, NT), 0) < lax.broadcasted_iota(jnp.int32, (NT, NT), 1),
        1.0, 0.0,
    ).astype(BF16)
    rank = jnp.dot(onehot_f.astype(BF16), before, preferred_element_type=F32)
    table = jnp.zeros((n_dev, 128), F32)
    for j in range(CAP):
        picks = jnp.where(rank == float(j), onehot_f, 0.0).astype(BF16)
        parts = []
        if j:
            parts.append(jnp.zeros((16 * j, NT), BF16))
        parts.append(vals)
        parts.append(jnp.zeros((128 - 16 * (j + 1), NT), BF16))
        table = table + nt_dot(picks, jnp.concatenate(parts, axis=0))
    t1[...] = table.reshape(NGY, NGX, NT_AX, 128)

    def exchange(phase, axis, pos, count, src_of, dst):
        def copy(d, to_or_from):
            return pltpu.make_async_remote_copy(
                src_ref=src_of(lax.rem(pos + d, count)),
                dst_ref=dst.at[to_or_from],
                send_sem=a_s.at[phase, d],
                recv_sem=a_r.at[phase, d],
                device_id={axis: lax.rem(pos + d, count)},
                device_id_type=MESH,
            )
        sent = [copy(d, pos) for d in range(1, count)]
        for c in sent:
            c.start()
        dst[pos] = src_of(pos)[...]
        return sent, [copy(d, lax.rem(pos + count - d, count)) for d in range(1, count)]

    s1, r1 = exchange(0, "gy", gy, NGY, lambda j: t1.at[j], b1)

    for c in loads:
        c.wait()

    def quarter(z, carry):
        q[z] = q[z] * 0.25
        return carry

    lane = lax.broadcasted_iota(jnp.int32, (CX, 128), 1)

    def pack_xy(k, f):
        px[k, 0] = f[:, PAD, :]
        px[k, 1] = f[:, PAD + CX - 1, :]
        packed = jnp.zeros((CX, 128), F32)
        for z in range(CZ):
            left = pltpu.roll(f[z, pl.ds(PAD, CX), 0:128], z, 1) if z else f[z, pl.ds(PAD, CX), 0:128]
            packed = jnp.where(lane == z, left, packed)
            right = pltpu.roll(f[z, pl.ds(PAD, CX), 128:256], 9 + z, 1)
            packed = jnp.where(lane == 8 + z, right, packed)
        turned = jnp.transpose(packed)
        py[k, 0] = turned[0:8]
        py[k, 1] = turned[8:16]
        for d in (0, 1):
            send(1, k, d, px.at[k, d])
            send(2, k, d, py.at[k, d])

    pack_xy(0, fa)
    lax.fori_loop(0, CZ, quarter, 0)

    for c in r1:
        c.wait_recv()
    s2, r2 = exchange(1, "gx", gx, NGX, lambda j: b1.at[:, j], b2)
    for c in r2:
        c.wait_recv()
    b2v = b2.reshape(NGX * NGY, NT_AX, 128)
    for j in range(NT_AX):
        b3[j] = b2v[:, j, :]
    s3, r3 = exchange(2, "trace", t, NT_AX, lambda j: b3.at[j], b4)
    for c in r3:
        c.wait_recv()

    nodes = b4[...].reshape(n_dev, 128)
    turned = jnp.transpose(nodes)
    row_of = []
    for j in range(CAP):
        zrow = turned[16 * j:16 * j + 1]
        xrow = turned[16 * j + 1:16 * j + 2]
        row_of.append((zrow * float(CX) + xrow).astype(jnp.int32))

    def fill_rows(z, carry):
        here = lax.broadcasted_iota(jnp.int32, (CX, 128), 0) + z * CX
        for j in range(CAP):
            rows_1h[pl.ds(pl.multiple_of(z * CX, CX), CX), j * 128:(j + 1) * 128] = jnp.where(
                here == row_of[j], 1.0, 0.0
            ).astype(BF16)
        return carry

    lax.fori_loop(0, CZ, fill_rows, 0)
    col_iota = lax.broadcasted_iota(jnp.int32, (n_dev, CY), 1)
    for j in range(CAP):
        ycol = nodes[:, 16 * j + 2:16 * j + 3].astype(jnp.int32)
        at_col = col_iota == ycol
        for s in range(STEPS):
            for v, off in ((v_hi, 3), (v_lo, 7)):
                v[s, j * 128:(j + 1) * 128, :] = jnp.where(
                    at_col, nodes[:, 16 * j + off + s:16 * j + off + s + 1], 0.0
                ).astype(BF16)

    def make_source(s):
        def one(z, carry):
            r = rows_1h[pl.ds(pl.multiple_of(z * CX, CX), CX), :]
            s_ref[z] = jnp.dot(r, v_hi[s], preferred_element_type=F32) + jnp.dot(
                r, v_lo[s], preferred_element_type=F32
            )
            return carry
        lax.fori_loop(0, CZ, one, 0)

    lane_r = lax.broadcasted_iota(jnp.int32, (ROWS, 128), 1)
    first, last = lane_r == 0, lane_r == 127

    def plane(k, cur, nxt, z, below, above):
        for r0 in range(0, CX, ROWS):
            rows = pl.ds(PAD + r0, ROWS)
            flat = pl.ds(r0, ROWS)
            h = hy[flat, :]
            h_lo = pltpu.roll(h, lax.rem(128 - z, 128), 1)
            h_hi = pltpu.roll(h, 119 - z, 1)
            mid = []
            for half in (0, 1):
                cols = slice(128 * half, 128 * half + 128)
                mid.append(cur[z, rows, cols])
            fwd = [pltpu.roll(m, 1, 1) for m in mid]
            bwd = [pltpu.roll(m, 127, 1) for m in mid]
            ym = [jnp.where(first, h_lo, fwd[0]), jnp.where(first, fwd[0], fwd[1])]
            yp = [jnp.where(last, bwd[1], bwd[0]), jnp.where(last, h_hi, bwd[1])]
            for half in (0, 1):
                cols = slice(128 * half, 128 * half + 128)
                beside = below(rows, flat, cols) + above(rows, flat, cols)
                beside = beside + (
                    cur[z, pl.ds(PAD + r0 - 1, ROWS), cols] + cur[z, pl.ds(PAD + r0 + 1, ROWS), cols]
                )
                beside = beside + (ym[half] + yp[half])
                m = mid[half]
                nxt[z, rows, cols] = (
                    2.0 * m
                    - nxt[z, rows, cols]
                    + q[z, flat, cols] * (beside - 6.0 * m + s_ref[z, flat, cols])
                )

    bufs = (fa, fb)
    outs = []
    make_source(0)
    for k in range(STEPS):
        cur, nxt = bufs[k % 2], bufs[(k + 1) % 2]
        wait_ghost(1, k)
        wait_ghost(2, k)
        cur[:, PAD - 1, :] = gx_buf[k, 0]
        cur[:, PAD + CX, :] = gx_buf[k, 1]
        both = jnp.concatenate(
            [gy_buf[k, 0], gy_buf[k, 1], jnp.zeros((112, CX), F32)], axis=0
        )
        hy[...] = jnp.transpose(both)

        def inner(z, carry, k=k, cur=cur, nxt=nxt):
            plane(
                k, cur, nxt, z,
                lambda rows, flat, cols: cur[z - 1, rows, cols],
                lambda rows, flat, cols: cur[z + 1, rows, cols],
            )
            return carry

        lax.fori_loop(1, CZ - 1, inner, 0)
        wait_ghost(0, k)
        if k >= 2:
            wait_sent(0, k - 1)
        plane(
            k, cur, nxt, 0,
            lambda rows, flat, cols: gz[k, 0, flat, cols],
            lambda rows, flat, cols: cur[1, rows, cols],
        )
        if k < STEPS - 1:
            send(0, k + 1, 0, nxt.at[0, pl.ds(PAD, CX), :])
        plane(
            k, cur, nxt, CZ - 1,
            lambda rows, flat, cols: cur[CZ - 2, rows, cols],
            lambda rows, flat, cols: gz[k, 1, flat, cols],
        )
        if k < STEPS - 1:
            send(0, k + 1, 1, nxt.at[CZ - 1, pl.ds(PAD, CX), :])
            pack_xy(k + 1, nxt)
            make_source(k + 1)
        if k == STEPS - 2:
            outs.append(pltpu.make_async_copy(nxt.at[:, pl.ds(PAD, CX), :], outp_hbm, osem.at[0]))
            outs[-1].start()
    outs.append(pltpu.make_async_copy(nxt.at[:, pl.ds(PAD, CX), :], outn_hbm, osem.at[1]))
    outs[-1].start()
    for c in s1 + s2 + s3:
        c.wait_send()
    for k in range(STEPS):
        for kind in range(3):
            if kind or k in (0, STEPS - 1):
                wait_sent(kind, k)
    for c in outs:
        c.wait()


def body(traces, coupling, tap_shift, node_tile, node_cell, field_prev, field_now, speed_sq):
    combined = jnp.sum(traces.astype(F32) * coupling.astype(F32)[:, :, None], axis=1)
    field = jax.ShapeDtypeStruct((CZ, CX, CY), F32)
    vmem = pl.BlockSpec(memory_space=pltpu.VMEM)
    hbm = pl.BlockSpec(memory_space=pl.ANY)
    dma = pltpu.SemaphoreType.DMA
    return pl.pallas_call(
        kernel,
        out_shape=(field, field),
        in_specs=[vmem] * 5 + [hbm] * 3,
        out_specs=(hbm, hbm),
        scratch_shapes=[
            pltpu.VMEM((CZ, CX + 2 * PAD, CY), F32),
            pltpu.VMEM((CZ, CX + 2 * PAD, CY), F32),
            pltpu.VMEM((CZ, CX, CY), F32),
            pltpu.VMEM((CZ, CX, CY), F32),
            pltpu.VMEM((STEPS, 2, CX, CY), F32),
            pltpu.VMEM((STEPS, 2, CZ, CY), F32),
            pltpu.VMEM((STEPS, 2, CZ, CX), F32),
            pltpu.VMEM((STEPS, 2, CZ, CY), F32),
            pltpu.VMEM((STEPS, 2, CZ, CX), F32),
            pltpu.VMEM((CX, 128), F32),
            pltpu.VMEM((CZ * CX, CAP * 128), BF16),
            pltpu.VMEM((STEPS, CAP * 128, CY), BF16),
            pltpu.VMEM((STEPS, CAP * 128, CY), BF16),
            pltpu.VMEM((NGY, NGX, NT_AX, 128), F32),
            pltpu.VMEM((NGY, NGX, NT_AX, 128), F32),
            pltpu.VMEM((NGX, NGY, NT_AX, 128), F32),
            pltpu.VMEM((NT_AX, NGX * NGY, 128), F32),
            pltpu.VMEM((NT_AX, NGX * NGY, 128), F32),
            dma((3,)),
            dma((2,)),
            dma((STEPS, 2)),
            dma((STEPS, 2)),
            dma((STEPS, 2)),
            dma((STEPS, 2)),
            dma((STEPS, 2)),
            dma((STEPS, 2)),
            dma((3, NT_AX)),
            dma((3, NT_AX)),
        ],
        compiler_params=pltpu.CompilerParams(collective_id=0, has_side_effects=True),
    )(
        combined,
        jnp.asarray(window_table()),
        tap_shift.reshape(1, -1),
        node_tile.reshape(1, -1),
        node_cell.reshape(1, -1),
        field_prev,
        field_now,
        speed_sq,
    )


def solution(mesh):
    everywhere = ("trace", "gx", "gy")
    placed = (
        P(everywhere, None, None),
        P(everywhere, None),
        P(everywhere),
        P(everywhere, None),
        P(everywhere),
        P("trace", "gx", "gy"),
        P("trace", "gx", "gy"),
        P("trace", "gx", "gy"),
    )
    return jax.shard_map(
        body,
        mesh=mesh,
        in_specs=placed,
        out_specs=(P("trace", "gx", "gy"), P("trace", "gx", "gy")),
        check_vma=False,
    )
```

profile of v0, /device:TPU:1, one launch (start us, length us, event | category | flops | bytes accessed | tf_op | source)
XLA Modules:
  0.0 53.2 jit_solution(14139163994713875113)
XLA Ops:
  0.6 0.8 %copy.11 = f32[256,4]{1,0:T(8,128)S(1)} copy(bf16[256,4]{0,1:T(4,128)(2,1)} %param.10) | data formatting | bytes 6144 | tf_op jit(solution)/shard_map/convert_element_type | solution.py:332
  1.4 2.5 %multiply_reduce_fusion.comb_ref = f32[256,256]{1,0:T(8,128)} fusion(bf16[256,4,256]{2,1,0:T(4,128)(2,1)} %param.9, f32[256,4]{1,0:T(8,128)S(1)} %copy.11), kind=kLoop, calls=%fused_computation | loop fusion | flops 720896 | bytes 790528 | tf_op jit(solution)/shard_map/reduce_sum | solution.py:332
  3.9 44.7 %shard_map.104 = (f32[8,256,256]{2,1,0:T(8,128)}, f32[8,256,256]{2,1,0:T(8,128)}) custom-call(f32[256,256]{1,0:T(8,128)} %multiply_reduce_fusion.comb_ref, f32[256,256]{1,0:T(8,128)} %constant.4.clone.win_ref, s32[1,256]{1,0:T(1,128)} %bitcast.3, s32[1,256]{1,0:T(1,128)} %bitcast.4, s32[1,256]{1,0:T(1,128)} %bitcast.5, f32[8,256,256]{2,1,0:T(8,128)} %prev_hbm.1, ...), custom_call_target="tpu_custom_call" | custom-call | tf_op jit(solution)/shard_map/pallas_call | solution.py:337
  48.7 0.0 copy-start
  48.7 3.2 %copy.14 = f32[8,256,256]{2,1,0:T(8,128)} copy(f32[8,256,256]{2,1,0:T(8,128)} %get-tuple-element.4) | data formatting | bytes 4194304
  51.9 0.0 copy-done
  51.9 1.3 %copy.15 = f32[8,256,256]{2,1,0:T(8,128)} copy(f32[8,256,256]{2,1,0:T(8,128)S(1)} %copy-done) | data formatting | bytes 4194304
Async XLA Ops:
  48.7 3.2 %copy-start = (f32[8,256,256]{2,1,0:T(8,128)S(1)}, f32[8,256,256]{2,1,0:T(8,128)}, u32[]{:S(2)}) copy-start(f32[8,256,256]{2,1,0:T(8,128)} %get-tuple-element.5) | copy-start | bytes 6291460
where the time goes:
time: 53.4 us; the launch traced here: 53.2 us
  Pallas kernels  44.7 us (84%)
  local copies, waits for them, and re-layouts  5.32 us (10%)
  other arithmetic  2.5 us (5%)
  between operations  0.65 us (1%)
    pallas_call x1, Pallas kernels, body(): pl.pallas_call(kernel, out_shape=(field, field), in_specs=[vmem] * 5 + [h...  44.7 us
    unnamed x4, local copies, waits for them, and re-layouts  4.52 us
    reduce_sum x1, other arithmetic, body(): jnp.sum(traces.astype(F32) * coupling.astype(F32)[:, :, None], axis=1)  2.5 us

commit v1 on v0

v1 whole, which is shorter than its diff:
```python
import math

import jax
import jax.numpy as jnp
import numpy as np
from jax import lax
from jax.experimental import pallas as pl
from jax.experimental.pallas import tpu as pltpu
from jax.sharding import PartitionSpec as P

NT = 256
STEPS = 4
RATE = 64
CZ, CX, CY = 8, 256, 256
NT_AX, NGX, NGY = 8, 4, 4
CAP = 4
COMP = 4
PAD = 8
ROWS = 32
MESH = pl.DeviceIdType.MESH
F32 = jnp.float32
BF16 = jnp.bfloat16


def window_table():
    u = (np.arange(NT)[None, :] + np.arange(NT)[:, None] - (NT - RATE // 2)).astype(np.float64)
    w = np.sinc(u / RATE) * 0.5 * (1.0 + np.cos(math.pi * u / (2.0 * RATE)))
    return np.where(np.abs(u) < 2.0 * RATE, w, 0.0).astype(np.float32)


def nt_dot(a, b, precision=None):
    return lax.dot_general(
        a, b, (((1,), (1,)), ((), ())), precision=precision, preferred_element_type=F32
    )


def kernel(
    traces_hbm, coup_ref, win_ref, shift_ref, tile_ref, cell_ref, prev_hbm, now_hbm, speed_hbm,
    outp_ref, outn_ref,
    tr, fa, fb, q, s_ref, gz, gx_buf, gy_buf, px, py, hy, rows_1h, v_hi, v_lo, t1, b4,
    lsem, osem, zs, zr, xs, xr, ys, yr, a_s, a_r,
):
    t = lax.axis_index("trace")
    gx = lax.axis_index("gx")
    gy = lax.axis_index("gy")
    n_dev = NT_AX * NGX * NGY
    me = (t * NGX + gx) * NGY + gy

    load_tr = pltpu.make_async_copy(traces_hbm, tr, lsem.at[3])
    load_tr.start()
    loads = [
        pltpu.make_async_copy(now_hbm, fa.at[:, pl.ds(PAD, CX), :], lsem.at[0]),
        pltpu.make_async_copy(prev_hbm, fb.at[:, pl.ds(PAD, CX), :], lsem.at[1]),
        pltpu.make_async_copy(speed_hbm, q, lsem.at[2]),
    ]
    for c in loads:
        c.start()

    def peer(d):
        k = lax.rem(me + d, n_dev)
        return k, (k // (NGX * NGY), lax.rem(k // NGY, NGX), lax.rem(k, NGY))

    barrier = pltpu.get_barrier_semaphore()

    def greet(d, carry):
        _, where = peer(d)
        pl.semaphore_signal(barrier, inc=1, device_id=where, device_id_type=MESH)
        return carry

    lax.fori_loop(1, n_dev, greet, 0)

    sides = (("trace", t, NT_AX), ("gx", gx, NGX), ("gy", gy, NGY))
    for buf, (_, pos, count) in zip((gz, gx_buf, gy_buf), sides):
        for side in (0, 1):
            @pl.when(pos == (0 if side == 0 else count - 1))
            def _(buf=buf, side=side):
                for k in range(STEPS):
                    buf[k, side] = jnp.zeros(buf.shape[2:], F32)

    def halo(kind, k, d, src=None):
        axis, pos, count = sides[kind]
        ghost = (gz, gx_buf, gy_buf)[kind]
        ssem, rsem = ((zs, zr), (xs, xr), (ys, yr))[kind]
        if src is None:
            src = ghost.at[k, 1 - d]
        to = jnp.maximum(pos - 1, 0) if d == 0 else jnp.minimum(pos + 1, count - 1)
        return pltpu.make_async_remote_copy(
            src_ref=src,
            dst_ref=ghost.at[k, 1 - d],
            send_sem=ssem.at[k, d],
            recv_sem=rsem.at[k, 1 - d],
            device_id={axis: to},
            device_id_type=MESH,
        )

    def exists(kind, d):
        _, pos, count = sides[kind]
        return pos > 0 if d == 0 else pos < count - 1

    def send(kind, k, d, src):
        @pl.when(exists(kind, d))
        def _():
            halo(kind, k, d, src).start()

    def wait_ghost(kind, k):
        for side in (0, 1):
            @pl.when(exists(kind, side))
            def _(side=side):
                halo(kind, k, 1 - side).wait_recv()

    def wait_sent(kind, k):
        for d in (0, 1):
            @pl.when(exists(kind, d))
            def _(d=d):
                halo(kind, k, d).wait_send()

    coup = jnp.transpose(
        jnp.concatenate([coup_ref[...].astype(F32), jnp.zeros((128 - COMP, NT), F32)], axis=0)
    )
    lane_i = lax.broadcasted_iota(jnp.int32, (NT, 128), 1)
    node_i = lax.broadcasted_iota(jnp.int32, (NT, 128), 0)
    comp = lane_i % COMP
    weight = coup[:, COMP - 1:COMP]
    for c in range(COMP - 2, -1, -1):
        weight = jnp.where(comp == c, coup[:, c:c + 1], weight)
    weight = jnp.where(lane_i // COMP == node_i % 32, weight, 0.0).astype(BF16)
    load_tr.wait()
    flat_tr = tr.reshape(NT * COMP, NT)
    combined = jnp.concatenate(
        [
            jnp.dot(
                weight[b * 32:(b + 1) * 32, :], flat_tr[b * 128:(b + 1) * 128, :],
                preferred_element_type=F32,
            )
            for b in range(NT // 32)
        ],
        axis=0,
    )

    at = nt_dot(win_ref[...], combined, lax.Precision.HIGHEST)
    shift = shift_ref[...]
    picked = lax.broadcasted_iota(jnp.int32, (RATE, NT), 0) == shift
    amps = [
        jnp.sum(jnp.where(picked, at[s * RATE:(s + 1) * RATE, :], 0.0), axis=0, keepdims=True)
        for s in range(STEPS)
    ]
    cell = cell_ref[...]
    cz = (cell // (CX * CY)).astype(F32)
    cx = ((cell // CY) % CX).astype(F32)
    cy = (cell % CY).astype(F32)
    hi = [a.astype(BF16).astype(F32) for a in amps]
    lo = [a - h for a, h in zip(amps, hi)]
    zero_row = jnp.zeros((1, NT), F32)
    vals = jnp.concatenate([cz, cx, cy] + hi + lo + [zero_row] * 5, axis=0).astype(BF16)
    onehot = lax.broadcasted_iota(jnp.int32, (n_dev, NT), 0) == tile_ref[...]
    onehot_f = jnp.where(onehot, 1.0, 0.0)
    before = jnp.where(
        lax.broadcasted_iota(jnp.int32, (NT, NT), 0) < lax.broadcasted_iota(jnp.int32, (NT, NT), 1),
        1.0, 0.0,
    ).astype(BF16)
    rank = jnp.dot(onehot_f.astype(BF16), before, preferred_element_type=F32)
    table = jnp.zeros((n_dev, 128), F32)
    for j in range(CAP):
        picks = jnp.where(rank == float(j), onehot_f, 0.0).astype(BF16)
        parts = []
        if j:
            parts.append(jnp.zeros((16 * j, NT), BF16))
        parts.append(vals)
        parts.append(jnp.zeros((128 - 16 * (j + 1), NT), BF16))
        table = table + nt_dot(picks, jnp.concatenate(parts, axis=0))
    t1[...] = table.reshape(n_dev, 1, 128)

    pl.semaphore_wait(barrier, n_dev - 1)

    def post(d, carry):
        k, where = peer(d)
        pltpu.make_async_remote_copy(
            src_ref=t1.at[k],
            dst_ref=b4.at[me],
            send_sem=a_s.at[0],
            recv_sem=a_r.at[0],
            device_id=where,
            device_id_type=MESH,
        ).start()
        return carry

    lax.fori_loop(1, n_dev, post, 0)
    b4[me] = t1[me]
    all_rows = pltpu.make_async_remote_copy(
        src_ref=t1.at[pl.ds(0, n_dev - 1)],
        dst_ref=b4.at[pl.ds(0, n_dev - 1)],
        send_sem=a_s.at[0],
        recv_sem=a_r.at[0],
        device_id=peer(1)[1],
        device_id_type=MESH,
    )

    send(0, 0, 0, now_hbm.at[0])
    send(0, 0, 1, now_hbm.at[CZ - 1])

    lane = lax.broadcasted_iota(jnp.int32, (CX, 128), 1)

    def pack_xy(k, f):
        px[k, 0] = f[:, PAD, :]
        px[k, 1] = f[:, PAD + CX - 1, :]
        packed = jnp.zeros((CX, 128), F32)
        for z in range(CZ):
            left = pltpu.roll(f[z, pl.ds(PAD, CX), 0:128], z, 1) if z else f[z, pl.ds(PAD, CX), 0:128]
            packed = jnp.where(lane == z, left, packed)
            right = pltpu.roll(f[z, pl.ds(PAD, CX), 128:256], 9 + z, 1)
            packed = jnp.where(lane == 8 + z, right, packed)
        turned = jnp.transpose(packed)
        py[k, 0] = turned[0:8]
        py[k, 1] = turned[8:16]
        for d in (0, 1):
            send(1, k, d, px.at[k, d])
            send(2, k, d, py.at[k, d])

    for c in loads:
        c.wait()
    pack_xy(0, fa)

    def quarter(z, carry):
        q[z] = q[z] * 0.25
        return carry

    lax.fori_loop(0, CZ, quarter, 0)

    def make_source(s):
        def one(i, carry):
            r = rows_1h[pl.ds(pl.multiple_of(i * 2 * CX, 2 * CX), 2 * CX), :]
            total = jnp.dot(r, v_hi[s], preferred_element_type=F32) + jnp.dot(
                r, v_lo[s], preferred_element_type=F32
            )
            s_ref[pl.ds(i * 2, 2)] = total.reshape(2, CX, CY)
            return carry
        lax.fori_loop(0, CZ // 2, one, 0)

    lane_r = lax.broadcasted_iota(jnp.int32, (ROWS, 128), 1)
    first, last = lane_r == 0, lane_r == 127

    def plane(cur, old, dst, dst_pad, z, below, above, source):
        for r0 in range(0, CX, ROWS):
            rows = pl.ds(PAD + r0, ROWS)
            flat = pl.ds(r0, ROWS)
            h = hy[flat, :]
            h_lo = pltpu.roll(h, lax.rem(128 - z, 128), 1)
            h_hi = pltpu.roll(h, 119 - z, 1)
            mid = []
            for half in (0, 1):
                cols = slice(128 * half, 128 * half + 128)
                mid.append(cur[z, rows, cols])
            fwd = [pltpu.roll(m, 1, 1) for m in mid]
            bwd = [pltpu.roll(m, 127, 1) for m in mid]
            ym = [jnp.where(first, h_lo, fwd[0]), jnp.where(first, fwd[0], fwd[1])]
            yp = [jnp.where(last, bwd[1], bwd[0]), jnp.where(last, h_hi, bwd[1])]
            for half in (0, 1):
                cols = slice(128 * half, 128 * half + 128)
                beside = below(rows, flat, cols) + above(rows, flat, cols)
                beside = beside + (
                    cur[z, pl.ds(PAD + r0 - 1, ROWS), cols] + cur[z, pl.ds(PAD + r0 + 1, ROWS), cols]
                )
                beside = beside + (ym[half] + yp[half])
                m = mid[half]
                beside = beside - 6.0 * m
                if source:
                    beside = beside + s_ref[z, flat, cols]
                dst[z, pl.ds(dst_pad + r0, ROWS), cols] = (
                    2.0 * m - old[z, rows, cols] + q[z, flat, cols] * beside
                )

    def ghosts_xy(k, cur):
        wait_ghost(1, k)
        wait_ghost(2, k)
        cur[:, PAD - 1, :] = gx_buf[k, 0]
        cur[:, PAD + CX, :] = gx_buf[k, 1]
        both = jnp.concatenate(
            [gy_buf[k, 0], gy_buf[k, 1], jnp.zeros((112, CX), F32)], axis=0
        )
        hy[...] = jnp.transpose(both)

    def inner_planes(cur, old, dst, dst_pad, source):
        def inner(z, carry):
            plane(
                cur, old, dst, dst_pad, z,
                lambda rows, flat, cols: cur[z - 1, rows, cols],
                lambda rows, flat, cols: cur[z + 1, rows, cols],
                source,
            )
            return carry

        lax.fori_loop(1, CZ - 1, inner, 0)

    def low_plane(k, cur, old, dst, dst_pad, source):
        plane(
            cur, old, dst, dst_pad, 0,
            lambda rows, flat, cols: gz[k, 0, flat, cols],
            lambda rows, flat, cols: cur[1, rows, cols],
            source,
        )

    def high_plane(k, cur, old, dst, dst_pad, source):
        plane(
            cur, old, dst, dst_pad, CZ - 1,
            lambda rows, flat, cols: cur[CZ - 2, rows, cols],
            lambda rows, flat, cols: gz[k, 1, flat, cols],
            source,
        )

    ghosts_xy(0, fa)
    inner_planes(fa, fb, fb, PAD, False)
    wait_ghost(0, 0)
    low_plane(0, fa, fb, fb, PAD, False)
    high_plane(0, fa, fb, fb, PAD, False)

    all_rows.wait_recv()

    nodes = b4[...].reshape(n_dev, 128)
    turned = jnp.transpose(nodes)
    row_of = []
    for j in range(CAP):
        zrow = turned[16 * j:16 * j + 1]
        xrow = turned[16 * j + 1:16 * j + 2]
        row_of.append((zrow * float(CX) + xrow).astype(jnp.int32))

    def fill_rows(z, carry):
        here = lax.broadcasted_iota(jnp.int32, (CX, 128), 0) + z * CX
        for j in range(CAP):
            rows_1h[pl.ds(pl.multiple_of(z * CX, CX), CX), j * 128:(j + 1) * 128] = jnp.where(
                here == row_of[j], 1.0, 0.0
            ).astype(BF16)
        return carry

    lax.fori_loop(0, CZ, fill_rows, 0)
    col_iota = lax.broadcasted_iota(jnp.int32, (n_dev, CY), 1)
    for j in range(CAP):
        ycol = nodes[:, 16 * j + 2:16 * j + 3].astype(jnp.int32)
        at_col = col_iota == ycol
        for s in range(STEPS):
            for v, off in ((v_hi, 3), (v_lo, 7)):
                v[s, j * 128:(j + 1) * 128, :] = jnp.where(
                    at_col, nodes[:, 16 * j + off + s:16 * j + off + s + 1], 0.0
                ).astype(BF16)

    make_source(0)

    def add_source(z, carry):
        rows = pl.ds(PAD, CX)
        fb[z, rows, :] = fb[z, rows, :] + q[z] * s_ref[z]
        return carry

    def send_z(k, f):
        send(0, k, 0, f.at[0, pl.ds(PAD, CX), :])
        send(0, k, 1, f.at[CZ - 1, pl.ds(PAD, CX), :])

    add_source(0, 0)
    add_source(CZ - 1, 0)
    send_z(1, fb)
    lax.fori_loop(1, CZ - 1, add_source, 0)
    pack_xy(1, fb)
    make_source(1)

    for k, cur, nxt in ((1, fb, fa), (2, fa, fb)):
        ghosts_xy(k, cur)
        inner_planes(cur, nxt, nxt, PAD, True)
        wait_ghost(0, k)
        if k >= 2:
            wait_sent(0, k - 1)
        low_plane(k, cur, nxt, nxt, PAD, True)
        high_plane(k, cur, nxt, nxt, PAD, True)
        send_z(k + 1, nxt)
        pack_xy(k + 1, nxt)
        make_source(k + 1)

    copy_prev = pltpu.make_async_copy(fb.at[:, pl.ds(PAD, CX), :], outp_ref, osem.at[0])
    copy_prev.start()
    ghosts_xy(3, fb)
    inner_planes(fb, fa, outn_ref, 0, True)
    wait_ghost(0, 3)
    low_plane(3, fb, fa, outn_ref, 0, True)
    high_plane(3, fb, fa, outn_ref, 0, True)

    all_rows.wait_send()
    for k in range(STEPS):
        for kind in range(3):
            if kind or k != 1:
                wait_sent(kind, k)
    copy_prev.wait()


def body(traces, coupling, tap_shift, node_tile, node_cell, field_prev, field_now, speed_sq):
    vmem = pl.BlockSpec(memory_space=pltpu.VMEM)
    hbm = pl.BlockSpec(memory_space=pltpu.HBM)
    dma = pltpu.SemaphoreType.DMA
    n_dev = NT_AX * NGX * NGY
    return pl.pallas_call(
        kernel,
        out_shape=(pltpu.VMEM((CZ, CX, CY), F32), pltpu.VMEM((CZ, CX, CY), F32)),
        in_specs=[hbm] + [vmem] * 5 + [hbm] * 3,
        out_specs=(vmem, vmem),
        scratch_shapes=[
            pltpu.VMEM((NT, COMP, NT), BF16),
            pltpu.VMEM((CZ, CX + 2 * PAD, CY), F32),
            pltpu.VMEM((CZ, CX + 2 * PAD, CY), F32),
            pltpu.VMEM((CZ, CX, CY), F32),
            pltpu.VMEM((CZ, CX, CY), F32),
            pltpu.VMEM((STEPS, 2, CX, CY), F32),
            pltpu.VMEM((STEPS, 2, CZ, CY), F32),
            pltpu.VMEM((STEPS, 2, CZ, CX), F32),
            pltpu.VMEM((STEPS, 2, CZ, CY), F32),
            pltpu.VMEM((STEPS, 2, CZ, CX), F32),
            pltpu.VMEM((CX, 128), F32),
            pltpu.VMEM((CZ * CX, CAP * 128), BF16),
            pltpu.VMEM((STEPS, CAP * 128, CY), BF16),
            pltpu.VMEM((STEPS, CAP * 128, CY), BF16),
            pltpu.VMEM((n_dev, 1, 128), F32),
            pltpu.VMEM((n_dev, 1, 128), F32),
            dma((4,)),
            dma((1,)),
            dma((STEPS, 2)),
            dma((STEPS, 2)),
            dma((STEPS, 2)),
            dma((STEPS, 2)),
            dma((STEPS, 2)),
            dma((STEPS, 2)),
            dma((1,)),
            dma((1,)),
        ],
        compiler_params=pltpu.CompilerParams(
            collective_id=0, has_side_effects=True, vmem_limit_bytes=62_400_000
        ),
    )(
        traces,
        coupling.T,
        jnp.asarray(window_table()),
        tap_shift.reshape(1, -1),
        node_tile.reshape(1, -1),
        node_cell.reshape(1, -1),
        field_prev,
        field_now,
        speed_sq,
    )


def solution(mesh):
    everywhere = ("trace", "gx", "gy")
    placed = (
        P(everywhere, None, None),
        P(everywhere, None),
        P(everywhere),
        P(everywhere, None),
        P(everywhere),
        P("trace", "gx", "gy"),
        P("trace", "gx", "gy"),
        P("trace", "gx", "gy"),
    )
    return jax.shard_map(
        body,
        mesh=mesh,
        in_specs=placed,
        out_specs=(P("trace", "gx", "gy"), P("trace", "gx", "gy")),
        check_vma=False,
    )
```

time: 53.4 us -> 49.2 us (0.921)
  local copies, waits for them, and re-layouts: 5.32 us -> 2.64 us
  other arithmetic: 2.5 us -> 0 us
  Pallas kernels: 44.7 us -> 45.8 us
    reduce_sum x1 -> x0, other arithmetic: 2.5 us -> none  [body(): jnp.sum(traces.astype(F32) * coupling.astype(F32)[:, :, None], axis=1)]
    unnamed x4 -> x2, local copies, waits for them, and re-layouts: 4.52 us -> 2.64 us
    pallas_call x1, Pallas kernels: 44.7 us -> 45.8 us  [body(): pl.pallas_call(kernel, out_shape=(pltpu.VMEM((CZ, CX, CY), F32), pltpu.VM...]
    convert_element_type x1 -> x0, local copies, waits for them, and re-layouts: 0.8 us -> none  [body(): coupling.astype(F32)[:, :, None]]
where the time goes in v1:
time: 49.2 us; the launch traced here: 49.1 us
  Pallas kernels  45.8 us (93%)
  local copies, waits for them, and re-layouts  2.64 us (5%)
  between operations  0.64 us (1%)
    pallas_call x1, Pallas kernels, body(): pl.pallas_call(kernel, out_shape=(pltpu.VMEM((CZ, CX, CY), F32), pltpu.VM...  45.8 us
    unnamed x2, local copies, waits for them, and re-layouts  2.64 us

profile of v1, /device:TPU:1, one launch (start us, length us, event | category | flops | bytes accessed | tf_op | source)
XLA Modules:
  0.0 49.1 jit_solution(3669798284796947352)
XLA Ops:
  0.6 45.8 %shard_map.104 = (f32[8,256,256]{2,1,0:T(8,128)S(1)}, f32[8,256,256]{2,1,0:T(8,128)S(1)}) custom-call(bf16[256,4,256]{2,1,0:T(4,128)(2,1)} %traces_hbm.1, bf16[4,256]{1,0:T(4,128)(2,1)} %bitcast.4, f32[256,256]{1,0:T(8,128)} %constant.2.clone.win_ref, s32[1,256]{1,0:T(1,128)} %bitcast.5, s32[1,256]{1,0:T(1,128)} %bitcast.6, s32[1,256]{1,0:T(1,128)} %bitcast.7, ...), custom_call_target="tpu_custom_call" | custom-call | tf_op jit(solution)/shard_map/pallas_call | solution.py:396
  46.4 1.3 %copy.13 = f32[8,256,256]{2,1,0:T(8,128)} copy(f32[8,256,256]{2,1,0:T(8,128)S(1)} %get-tuple-element.2) | data formatting | bytes 4194304
  47.8 1.3 %copy.14 = f32[8,256,256]{2,1,0:T(8,128)} copy(f32[8,256,256]{2,1,0:T(8,128)S(1)} %get-tuple-element.3) | data formatting | bytes 4194304

commit v2 on v1

--- a/solution.py
+++ b/solution.py
@@ -37,7 +37,7 @@
 def kernel(
     traces_hbm, coup_ref, win_ref, shift_ref, tile_ref, cell_ref, prev_hbm, now_hbm, speed_hbm,
     outp_ref, outn_ref,
-    tr, fa, fb, q, s_ref, gz, gx_buf, gy_buf, px, py, hy, rows_1h, v_hi, v_lo, t1, b4,
+    tr, fa, fb, q, s_ref, gz, gx_buf, gy_buf, px, py, hy, rows_1h, v_hi, v_lo, t1, b4, dense,
     lsem, osem, zs, zr, xs, xr, ys, yr, a_s, a_r,
 ):
     t = lax.axis_index("trace")
@@ -226,15 +226,27 @@
 
     lax.fori_loop(0, CZ, quarter, 0)
 
+    def scattered(s, r):
+        total = jnp.dot(r, v_hi[s], preferred_element_type=F32) + jnp.dot(
+            r, v_lo[s], preferred_element_type=F32
+        )
+        return total.reshape(2, CX, CY)
+
+    def source_ends(s):
+        both = scattered(s, jnp.concatenate([rows_1h[0:CX], rows_1h[(CZ - 1) * CX:CZ * CX]], axis=0))
+        s_ref[0] = both[0]
+        s_ref[CZ - 1] = both[1]
+
+    def source_inner(s):
+        def one(i, carry):
+            z = 2 * i + 1
+            s_ref[pl.ds(z, 2)] = scattered(s, rows_1h[pl.ds(pl.multiple_of(z * CX, CX), 2 * CX), :])
+            return carry
+        lax.fori_loop(0, CZ // 2 - 1, one, 0)
+
     def make_source(s):
-        def one(i, carry):
-            r = rows_1h[pl.ds(pl.multiple_of(i * 2 * CX, 2 * CX), 2 * CX), :]
-            total = jnp.dot(r, v_hi[s], preferred_element_type=F32) + jnp.dot(
-                r, v_lo[s], preferred_element_type=F32
-            )
-            s_ref[pl.ds(i * 2, 2)] = total.reshape(2, CX, CY)
-            return carry
-        lax.fori_loop(0, CZ // 2, one, 0)
+        source_ends(s)
+        source_inner(s)
 
     lane_r = lax.broadcasted_iota(jnp.int32, (ROWS, 128), 1)
     first, last = lane_r == 0, lane_r == 127
@@ -315,7 +327,8 @@
 
     all_rows.wait_recv()
 
-    nodes = b4[...].reshape(n_dev, 128)
+    dense[...] = b4[...].reshape(n_dev, 128)
+    nodes = dense[...]
     turned = jnp.transpose(nodes)
     row_of = []
     for j in range(CAP):
@@ -331,18 +344,17 @@
             ).astype(BF16)
         return carry
 
-    lax.fori_loop(0, CZ, fill_rows, 0)
     col_iota = lax.broadcasted_iota(jnp.int32, (n_dev, CY), 1)
-    for j in range(CAP):
-        ycol = nodes[:, 16 * j + 2:16 * j + 3].astype(jnp.int32)
-        at_col = col_iota == ycol
-        for s in range(STEPS):
-            for v, off in ((v_hi, 3), (v_lo, 7)):
-                v[s, j * 128:(j + 1) * 128, :] = jnp.where(
-                    at_col, nodes[:, 16 * j + off + s:16 * j + off + s + 1], 0.0
-                ).astype(BF16)
-
-    make_source(0)
+
+    def fill_values(s_list):
+        for j in range(CAP):
+            at_col = col_iota == dense[:, 16 * j + 2:16 * j + 3].astype(jnp.int32)
+            for s in s_list:
+                for v, off in ((v_hi, 3), (v_lo, 7)):
+                    c = 16 * j + off + s
+                    v[s, j * 128:(j + 1) * 128, :] = jnp.where(
+                        at_col, dense[:, c:c + 1], 0.0
+                    ).astype(BF16)
 
     def add_source(z, carry):
         rows = pl.ds(PAD, CX)
@@ -353,11 +365,18 @@
         send(0, k, 0, f.at[0, pl.ds(PAD, CX), :])
         send(0, k, 1, f.at[CZ - 1, pl.ds(PAD, CX), :])
 
+    fill_rows(0, 0)
+    fill_rows(CZ - 1, 0)
+    fill_values((0,))
+    source_ends(0)
     add_source(0, 0)
     add_source(CZ - 1, 0)
     send_z(1, fb)
+    lax.fori_loop(1, CZ - 1, fill_rows, 0)
+    source_inner(0)
     lax.fori_loop(1, CZ - 1, add_source, 0)
     pack_xy(1, fb)
+    fill_values((1, 2, 3))
     make_source(1)
 
     for k, cur, nxt in ((1, fb, fa), (2, fa, fb)):
@@ -388,12 +407,23 @@
     copy_prev.wait()
 
 
+def put_out(p_ref, n_ref, p_hbm, n_hbm, sem):
+    copies = [
+        pltpu.make_async_copy(p_ref, p_hbm, sem.at[0]),
+        pltpu.make_async_copy(n_ref, n_hbm, sem.at[1]),
+    ]
+    for c in copies:
+        c.start()
+    for c in copies:
+        c.wait()
+
+
 def body(traces, coupling, tap_shift, node_tile, node_cell, field_prev, field_now, speed_sq):
     vmem = pl.BlockSpec(memory_space=pltpu.VMEM)
     hbm = pl.BlockSpec(memory_space=pltpu.HBM)
     dma = pltpu.SemaphoreType.DMA
     n_dev = NT_AX * NGX * NGY
-    return pl.pallas_call(
+    last_two = pl.pallas_call(
         kernel,
         out_shape=(pltpu.VMEM((CZ, CX, CY), F32), pltpu.VMEM((CZ, CX, CY), F32)),
         in_specs=[hbm] + [vmem] * 5 + [hbm] * 3,
@@ -415,6 +445,7 @@
             pltpu.VMEM((STEPS, CAP * 128, CY), BF16),
             pltpu.VMEM((n_dev, 1, 128), F32),
             pltpu.VMEM((n_dev, 1, 128), F32),
+            pltpu.VMEM((n_dev, 128), F32),
             dma((4,)),
             dma((1,)),
             dma((STEPS, 2)),
@@ -440,6 +471,15 @@
         field_now,
         speed_sq,
     )
+    field = jax.ShapeDtypeStruct((CZ, CX, CY), F32)
+    return pl.pallas_call(
+        put_out,
+        out_shape=(field, field),
+        in_specs=[vmem] * 2,
+        out_specs=(hbm, hbm),
+        scratch_shapes=[dma((2,))],
+        compiler_params=pltpu.CompilerParams(vmem_limit_bytes=1024 * 1024),
+    )(*last_two)
 
 
 def solution(mesh):

time: 49.2 us -> 43.7 us (0.89)
  Pallas kernels: 45.8 us -> 42.9 us
  local copies, waits for them, and re-layouts: 2.64 us -> 0 us
    pallas_call x1, Pallas kernels: 45.8 us -> 40.9 us  [body(): pl.pallas_call(kernel, out_shape=(pltpu.VMEM((CZ, CX, CY), F32), pltpu.VM...]
    unnamed x2 -> x0, local copies, waits for them, and re-layouts: 2.64 us -> none
    pallas_call x0 -> x1, Pallas kernels: none -> 2.03 us  [body(): pl.pallas_call(put_out, out_shape=(field, field), in_specs=[vmem] * 2, ou...]
where the time goes in v2:
time: 43.7 us; the launch traced here: 43.5 us
  Pallas kernels  42.9 us (98%)
  between operations  0.64 us (1%)
    pallas_call x1, Pallas kernels, body(): pl.pallas_call(kernel, out_shape=(pltpu.VMEM((CZ, CX, CY), F32), pltpu.VM...  40.9 us
    pallas_call x1, Pallas kernels, body(): pl.pallas_call(put_out, out_shape=(field, field), in_specs=[vmem] * 2, ou...  2.03 us

profile of v2, /device:TPU:1, one launch (start us, length us, event | category | flops | bytes accessed | tf_op | source)
XLA Modules:
  0.0 43.5 jit_solution(1376154588393679274)
XLA Ops:
  0.6 40.9 %shard_map.104 = (f32[8,256,256]{2,1,0:T(8,128)S(1)}, f32[8,256,256]{2,1,0:T(8,128)S(1)}) custom-call(bf16[256,4,256]{2,1,0:T(4,128)(2,1)} %traces_hbm.1, bf16[4,256]{1,0:T(4,128)(2,1)} %bitcast.4, f32[256,256]{1,0:T(8,128)} %constant.2.clone.win_ref, s32[1,256]{1,0:T(1,128)} %bitcast.5, s32[1,256]{1,0:T(1,128)} %bitcast.6, s32[1,256]{1,0:T(1,128)} %bitcast.7, ...), custom_call_target="tpu_custom_call" | custom-call | tf_op jit(solution)/shard_map/pallas_call | solution.py:426
  41.5 2.0 %shard_map.105 = (f32[8,256,256]{2,1,0:T(8,128)}, f32[8,256,256]{2,1,0:T(8,128)}) custom-call(f32[8,256,256]{2,1,0:T(8,128)S(1)} %get-tuple-element.4.p_ref, f32[8,256,256]{2,1,0:T(8,128)S(1)} %get-tuple-element.5.n_ref), custom_call_target="tpu_custom_call" | custom-call | tf_op jit(solution)/shard_map/pallas_call | solution.py:475

commit v3 on v2

--- a/solution.py
+++ b/solution.py
@@ -37,8 +37,8 @@
 def kernel(
     traces_hbm, coup_ref, win_ref, shift_ref, tile_ref, cell_ref, prev_hbm, now_hbm, speed_hbm,
     outp_ref, outn_ref,
-    tr, fa, fb, q, s_ref, gz, gx_buf, gy_buf, px, py, hy, rows_1h, v_hi, v_lo, t1, b4, dense,
-    lsem, osem, zs, zr, xs, xr, ys, yr, a_s, a_r,
+    tr, fa, fb, q, s_even, s_odd, gz, gi, gs, fo, so, gx_buf, gy_buf, px, py, hy, rows_1h, v_hi, v_lo, t1, b4, dense,
+    lsem, osem, zs, zr, es, er, xs, xr, ys, yr, a_s, a_r,
 ):
     t = lax.axis_index("trace")
     gx = lax.axis_index("gx")
@@ -70,12 +70,13 @@
     lax.fori_loop(1, n_dev, greet, 0)
 
     sides = (("trace", t, NT_AX), ("gx", gx, NGX), ("gy", gy, NGY))
-    for buf, (_, pos, count) in zip((gz, gx_buf, gy_buf), sides):
+    zsides = (sides[0],) * 3 + sides[1:]
+    for buf, (_, pos, count) in zip((gz, gi, gs, gx_buf, gy_buf), zsides):
         for side in (0, 1):
             @pl.when(pos == (0 if side == 0 else count - 1))
             def _(buf=buf, side=side):
-                for k in range(STEPS):
-                    buf[k, side] = jnp.zeros(buf.shape[2:], F32)
+                for k in range(buf.shape[0]):
+                    buf[k, side] = jnp.zeros(buf.shape[2:], buf.dtype)
 
     def halo(kind, k, d, src=None):
         axis, pos, count = sides[kind]
@@ -83,15 +84,56 @@
         ssem, rsem = ((zs, zr), (xs, xr), (ys, yr))[kind]
         if src is None:
             src = ghost.at[k, 1 - d]
-        to = jnp.maximum(pos - 1, 0) if d == 0 else jnp.minimum(pos + 1, count - 1)
         return pltpu.make_async_remote_copy(
             src_ref=src,
             dst_ref=ghost.at[k, 1 - d],
             send_sem=ssem.at[k, d],
             recv_sem=rsem.at[k, 1 - d],
-            device_id={axis: to},
+            device_id={axis: jnp.clip(pos + 2 * d - 1, 0, count - 1)},
             device_id_type=MESH,
         )
+
+    def faces(k, d):
+        return [
+            pltpu.make_async_remote_copy(
+                src_ref=out.at[k - 1, d],
+                dst_ref=ghost.at[k - 1, 1 - d],
+                send_sem=ssem.at[k, d],
+                recv_sem=rsem.at[k, 1 - d],
+                device_id={"trace": jnp.clip(t + 2 * d - 1, 0, NT_AX - 1)},
+                device_id_type=MESH,
+            )
+            for out, ghost, ssem, rsem in ((fo, gi, zs, zr), (so, gs, es, er))
+        ]
+
+    def face_exists(d):
+        there = t + 2 * d - 1
+        return jnp.logical_and(there >= 0, there < NT_AX)
+
+    def send_face(k, d, f):
+        v = f[d * (CZ - 1), pl.ds(PAD, CX), :].reshape(CX // 8, 8, CY)
+        top = jnp.maximum(jnp.max(jnp.abs(v), axis=0), 1e-30)
+        code = (v * (32767.0 / top)[None] + 32768.5).astype(jnp.int32) - 32768
+        fo[k - 1, d] = code.reshape(CX, CY).astype(jnp.int16)
+        so[k - 1, d] = top * (1.0 / 32767.0)
+
+        @pl.when(face_exists(d))
+        def _():
+            for c in faces(k, d):
+                c.start()
+
+    def wait_face(k, side):
+        @pl.when(face_exists(side))
+        def _():
+            for c in faces(k, 1 - side):
+                c.wait_recv()
+
+    def wait_faces_sent(k):
+        for d in (0, 1):
+            @pl.when(face_exists(d))
+            def _(d=d):
+                for c in faces(k, d):
+                    c.wait_send()
 
     def exists(kind, d):
         _, pos, count = sides[kind]
@@ -200,7 +242,7 @@
 
     lane = lax.broadcasted_iota(jnp.int32, (CX, 128), 1)
 
-    def pack_xy(k, f):
+    def pack_xy(k, f, beside_it=None):
         px[k, 0] = f[:, PAD, :]
         px[k, 1] = f[:, PAD + CX - 1, :]
         packed = jnp.zeros((CX, 128), F32)
@@ -212,6 +254,8 @@
         turned = jnp.transpose(packed)
         py[k, 0] = turned[0:8]
         py[k, 1] = turned[8:16]
+        if beside_it is not None:
+            beside_it()
         for d in (0, 1):
             send(1, k, d, px.at[k, d])
             send(2, k, d, py.at[k, d])
@@ -232,21 +276,17 @@
         )
         return total.reshape(2, CX, CY)
 
+    sources = (s_even, s_odd)
+
     def source_ends(s):
         both = scattered(s, jnp.concatenate([rows_1h[0:CX], rows_1h[(CZ - 1) * CX:CZ * CX]], axis=0))
-        s_ref[0] = both[0]
-        s_ref[CZ - 1] = both[1]
-
-    def source_inner(s):
-        def one(i, carry):
-            z = 2 * i + 1
-            s_ref[pl.ds(z, 2)] = scattered(s, rows_1h[pl.ds(pl.multiple_of(z * CX, CX), 2 * CX), :])
-            return carry
-        lax.fori_loop(0, CZ // 2 - 1, one, 0)
-
-    def make_source(s):
-        source_ends(s)
-        source_inner(s)
+        sources[s % 2][0] = both[0]
+        sources[s % 2][CZ - 1] = both[1]
+
+    def source_pair(s, z):
+        sources[s % 2][pl.ds(z, 2)] = scattered(
+            s, rows_1h[pl.ds(pl.multiple_of(z * CX, CX), 2 * CX), :]
+        )
 
     lane_r = lax.broadcasted_iota(jnp.int32, (ROWS, 128), 1)
     first, last = lane_r == 0, lane_r == 127
@@ -275,8 +315,8 @@
                 beside = beside + (ym[half] + yp[half])
                 m = mid[half]
                 beside = beside - 6.0 * m
-                if source:
-                    beside = beside + s_ref[z, flat, cols]
+                if source is not None:
+                    beside = beside + source[z, flat, cols]
                 dst[z, pl.ds(dst_pad + r0, ROWS), cols] = (
                     2.0 * m - old[z, rows, cols] + q[z, flat, cols] * beside
                 )
@@ -291,39 +331,41 @@
         )
         hy[...] = jnp.transpose(both)
 
-    def inner_planes(cur, old, dst, dst_pad, source):
-        def inner(z, carry):
-            plane(
-                cur, old, dst, dst_pad, z,
-                lambda rows, flat, cols: cur[z - 1, rows, cols],
-                lambda rows, flat, cols: cur[z + 1, rows, cols],
-                source,
-            )
+    def inner_planes(cur, old, dst, dst_pad, source, ahead=None):
+        def inner(i, carry):
+            for z in (2 * i + 1, 2 * i + 2):
+                plane(
+                    cur, old, dst, dst_pad, z,
+                    lambda rows, flat, cols: cur[z - 1, rows, cols],
+                    lambda rows, flat, cols: cur[z + 1, rows, cols],
+                    source,
+                )
+            if ahead is not None:
+                source_pair(ahead, 2 * i + 1)
             return carry
 
-        lax.fori_loop(1, CZ - 1, inner, 0)
-
-    def low_plane(k, cur, old, dst, dst_pad, source):
+        lax.fori_loop(0, CZ // 2 - 1, inner, 0)
+
+    def end_plane(k, side, cur, old, dst, dst_pad, source):
+        def ghost(rows, flat, cols):
+            if k == 0:
+                return gz[0, side, flat, cols]
+            code = gi[k - 1, side, flat, cols].astype(jnp.int32).astype(F32)
+            scale = gs[k - 1, side, :, cols]
+            return (code.reshape(ROWS // 8, 8, 128) * scale[None]).reshape(ROWS, 128)
+
         plane(
-            cur, old, dst, dst_pad, 0,
-            lambda rows, flat, cols: gz[k, 0, flat, cols],
-            lambda rows, flat, cols: cur[1, rows, cols],
+            cur, old, dst, dst_pad, side * (CZ - 1),
+            ghost,
+            lambda rows, flat, cols: cur[1 + side * (CZ - 3), rows, cols],
             source,
         )
 
-    def high_plane(k, cur, old, dst, dst_pad, source):
-        plane(
-            cur, old, dst, dst_pad, CZ - 1,
-            lambda rows, flat, cols: cur[CZ - 2, rows, cols],
-            lambda rows, flat, cols: gz[k, 1, flat, cols],
-            source,
-        )
-
     ghosts_xy(0, fa)
-    inner_planes(fa, fb, fb, PAD, False)
+    inner_planes(fa, fb, fb, PAD, None)
     wait_ghost(0, 0)
-    low_plane(0, fa, fb, fb, PAD, False)
-    high_plane(0, fa, fb, fb, PAD, False)
+    end_plane(0, 0, fa, fb, fb, PAD, None)
+    end_plane(0, 1, fa, fb, fb, PAD, None)
 
     all_rows.wait_recv()
 
@@ -356,54 +398,56 @@
                         at_col, dense[:, c:c + 1], 0.0
                     ).astype(BF16)
 
-    def add_source(z, carry):
-        rows = pl.ds(PAD, CX)
-        fb[z, rows, :] = fb[z, rows, :] + q[z] * s_ref[z]
-        return carry
-
-    def send_z(k, f):
-        send(0, k, 0, f.at[0, pl.ds(PAD, CX), :])
-        send(0, k, 1, f.at[CZ - 1, pl.ds(PAD, CX), :])
-
     fill_rows(0, 0)
     fill_rows(CZ - 1, 0)
     fill_values((0,))
     source_ends(0)
-    add_source(0, 0)
-    add_source(CZ - 1, 0)
-    send_z(1, fb)
+    for side in (0, 1):
+        z = side * (CZ - 1)
+        fb[z, pl.ds(PAD, CX), :] = fb[z, pl.ds(PAD, CX), :] + q[z] * s_even[z]
+        send_face(1, side, fb)
     lax.fori_loop(1, CZ - 1, fill_rows, 0)
-    source_inner(0)
-    lax.fori_loop(1, CZ - 1, add_source, 0)
-    pack_xy(1, fb)
     fill_values((1, 2, 3))
-    make_source(1)
-
-    for k, cur, nxt in ((1, fb, fa), (2, fa, fb)):
+
+    def first_sources(i, carry):
+        z = 2 * i + 1
+        r = rows_1h[pl.ds(pl.multiple_of(z * CX, CX), 2 * CX), :]
+        now = scattered(0, r)
+        for n in (0, 1):
+            fb[z + n, pl.ds(PAD, CX), :] = fb[z + n, pl.ds(PAD, CX), :] + q[z + n] * now[n]
+        s_odd[pl.ds(z, 2)] = scattered(1, r)
+        return carry
+
+    lax.fori_loop(0, CZ // 2 - 1, first_sources, 0)
+    pack_xy(1, fb, lambda: source_ends(1))
+
+    off_chip = lax.rem(t, 2)
+    for k in range(1, STEPS):
+        cur = fb if k % 2 else fa
+        nxt = fa if k % 2 else fb
+        final = k == STEPS - 1
+        dst, dst_pad = (outn_ref, 0) if final else (nxt, PAD)
+        source = sources[k % 2]
+        if final:
+            copy_prev = pltpu.make_async_copy(cur.at[:, pl.ds(PAD, CX), :], outp_ref, osem.at[0])
+            copy_prev.start()
         ghosts_xy(k, cur)
-        inner_planes(cur, nxt, nxt, PAD, True)
-        wait_ghost(0, k)
-        if k >= 2:
-            wait_sent(0, k - 1)
-        low_plane(k, cur, nxt, nxt, PAD, True)
-        high_plane(k, cur, nxt, nxt, PAD, True)
-        send_z(k + 1, nxt)
-        pack_xy(k + 1, nxt)
-        make_source(k + 1)
-
-    copy_prev = pltpu.make_async_copy(fb.at[:, pl.ds(PAD, CX), :], outp_ref, osem.at[0])
-    copy_prev.start()
-    ghosts_xy(3, fb)
-    inner_planes(fb, fa, outn_ref, 0, True)
-    wait_ghost(0, 3)
-    low_plane(3, fb, fa, outn_ref, 0, True)
-    high_plane(3, fb, fa, outn_ref, 0, True)
+        inner_planes(cur, nxt, dst, dst_pad, source, None if final else k + 1)
+        for side in (1 - off_chip, off_chip):
+            wait_face(k, side)
+            end_plane(k, side, cur, nxt, dst, dst_pad, source)
+            if not final:
+                send_face(k + 1, side, nxt)
+        if not final:
+            pack_xy(k + 1, nxt, lambda: source_ends(k + 1))
 
     all_rows.wait_send()
+    wait_sent(0, 0)
     for k in range(STEPS):
-        for kind in range(3):
-            if kind or k != 1:
-                wait_sent(kind, k)
+        wait_sent(1, k)
+        wait_sent(2, k)
+        if k:
+            wait_faces_sent(k)
     copy_prev.wait()
 
 
@@ -434,7 +478,12 @@
             pltpu.VMEM((CZ, CX + 2 * PAD, CY), F32),
             pltpu.VMEM((CZ, CX, CY), F32),
             pltpu.VMEM((CZ, CX, CY), F32),
-            pltpu.VMEM((STEPS, 2, CX, CY), F32),
+            pltpu.VMEM((CZ, CX, CY), F32),
+            pltpu.VMEM((1, 2, CX, CY), F32),
+            pltpu.VMEM((STEPS - 1, 2, CX, CY), jnp.int16),
+            pltpu.VMEM((STEPS - 1, 2, 8, CY), F32),
+            pltpu.VMEM((STEPS - 1, 2, CX, CY), jnp.int16),
+            pltpu.VMEM((STEPS - 1, 2, 8, CY), F32),
             pltpu.VMEM((STEPS, 2, CZ, CY), F32),
             pltpu.VMEM((STEPS, 2, CZ, CX), F32),
             pltpu.VMEM((STEPS, 2, CZ, CY), F32),
@@ -448,6 +497,8 @@
             pltpu.VMEM((n_dev, 128), F32),
             dma((4,)),
             dma((1,)),
+            dma((STEPS, 2)),
+            dma((STEPS, 2)),
             dma((STEPS, 2)),
             dma((STEPS, 2)),
             dma((STEPS, 2)),

time: 43.7 us -> 43.7 us (level)
  no operation moved by 1% of the time
where the time goes in v3:
time: 43.7 us; the launch traced here: 43.6 us
  Pallas kernels  43 us (98%)
  between operations  0.64 us (1%)
    pallas_call x1, Pallas kernels, body(): pl.pallas_call(kernel, out_shape=(pltpu.VMEM((CZ, CX, CY), F32), pltpu.VM...  40.9 us
    pallas_call x1, Pallas kernels, body(): pl.pallas_call(put_out, out_shape=(field, field), in_specs=[vmem] * 2, ou...  2.03 us

profile of v3, /device:TPU:1, one launch (start us, length us, event | category | flops | bytes accessed | tf_op | source)
XLA Modules:
  0.0 43.6 jit_solution(3628171624288478631)
XLA Ops:
  0.6 40.9 %shard_map.104 = (f32[8,256,256]{2,1,0:T(8,128)S(1)}, f32[8,256,256]{2,1,0:T(8,128)S(1)}) custom-call(bf16[256,4,256]{2,1,0:T(4,128)(2,1)} %traces_hbm.1, bf16[4,256]{1,0:T(4,128)(2,1)} %bitcast.4, f32[256,256]{1,0:T(8,128)} %constant.2.clone.win_ref, s32[1,256]{1,0:T(1,128)} %bitcast.5, s32[1,256]{1,0:T(1,128)} %bitcast.6, s32[1,256]{1,0:T(1,128)} %bitcast.7, ...), custom_call_target="tpu_custom_call" | custom-call | tf_op jit(solution)/shard_map/pallas_call | solution.py:470
  41.6 2.0 %shard_map.105 = (f32[8,256,256]{2,1,0:T(8,128)}, f32[8,256,256]{2,1,0:T(8,128)}) custom-call(f32[8,256,256]{2,1,0:T(8,128)S(1)} %get-tuple-element.4.p_ref, f32[8,256,256]{2,1,0:T(8,128)S(1)} %get-tuple-element.5.n_ref), custom_call_target="tpu_custom_call" | custom-call | tf_op jit(solution)/shard_map/pallas_call | solution.py:526

commit v4 on v3

--- a/solution.py
+++ b/solution.py
@@ -48,6 +48,9 @@
 
     load_tr = pltpu.make_async_copy(traces_hbm, tr, lsem.at[3])
     load_tr.start()
+    for f in (fa, fb):
+        for row in (PAD - 1, PAD + CX):
+            f[:, row:row + 1, :] = jnp.zeros((CZ, 1, CY), F32)
     loads = [
         pltpu.make_async_copy(now_hbm, fa.at[:, pl.ds(PAD, CX), :], lsem.at[0]),
         pltpu.make_async_copy(prev_hbm, fb.at[:, pl.ds(PAD, CX), :], lsem.at[1]),
@@ -242,27 +245,31 @@
 
     lane = lax.broadcasted_iota(jnp.int32, (CX, 128), 1)
 
-    def pack_xy(k, f, beside_it=None):
-        px[k, 0] = f[:, PAD, :]
-        px[k, 1] = f[:, PAD + CX - 1, :]
+    parts_of = (tuple(range(1, CZ - 1)), (0, CZ - 1))
+
+    def pack_xy(k, part, f, beside_it=None):
+        n = 2 * k + part
+        px[n, 0] = f[:, PAD, :]
+        px[n, 1] = f[:, PAD + CX - 1, :]
         packed = jnp.zeros((CX, 128), F32)
-        for z in range(CZ):
+        for z in parts_of[part]:
             left = pltpu.roll(f[z, pl.ds(PAD, CX), 0:128], z, 1) if z else f[z, pl.ds(PAD, CX), 0:128]
             packed = jnp.where(lane == z, left, packed)
             right = pltpu.roll(f[z, pl.ds(PAD, CX), 128:256], 9 + z, 1)
             packed = jnp.where(lane == 8 + z, right, packed)
         turned = jnp.transpose(packed)
-        py[k, 0] = turned[0:8]
-        py[k, 1] = turned[8:16]
+        py[n, 0] = turned[0:8]
+        py[n, 1] = turned[8:16]
         if beside_it is not None:
             beside_it()
         for d in (0, 1):
-            send(1, k, d, px.at[k, d])
-            send(2, k, d, py.at[k, d])
+            send(1, n, d, px.at[n, d])
+            send(2, n, d, py.at[n, d])
 
     for c in loads:
         c.wait()
-    pack_xy(0, fa)
+    pack_xy(0, 0, fa)
+    pack_xy(0, 1, fa)
 
     def quarter(z, carry):
         q[z] = q[z] * 0.25
@@ -291,13 +298,16 @@
     lane_r = lax.broadcasted_iota(jnp.int32, (ROWS, 128), 1)
     first, last = lane_r == 0, lane_r == 127
 
-    def plane(cur, old, dst, dst_pad, z, below, above, source):
+    def plane(part, cur, old, dst, dst_pad, z, below, above, source):
         for r0 in range(0, CX, ROWS):
             rows = pl.ds(PAD + r0, ROWS)
             flat = pl.ds(r0, ROWS)
-            h = hy[flat, :]
-            h_lo = pltpu.roll(h, lax.rem(128 - z, 128), 1)
-            h_hi = pltpu.roll(h, 119 - z, 1)
+            if part:
+                h = hy[part, flat, :]
+                h_lo = pltpu.roll(h, lax.rem(128 - z, 128), 1)
+                h_hi = pltpu.roll(h, 119 - z, 1)
+            else:
+                h_lo = h_hi = 0.0
             mid = []
             for half in (0, 1):
                 cols = slice(128 * half, 128 * half + 128)
@@ -321,21 +331,24 @@
                     2.0 * m - old[z, rows, cols] + q[z, flat, cols] * beside
                 )
 
-    def ghosts_xy(k, cur):
-        wait_ghost(1, k)
-        wait_ghost(2, k)
-        cur[:, PAD - 1, :] = gx_buf[k, 0]
-        cur[:, PAD + CX, :] = gx_buf[k, 1]
+    def ghosts_xy(k, part, cur):
+        n = 2 * k + part
+        wait_ghost(1, n)
+        wait_ghost(2, n)
+        if part:
+            for z in parts_of[part]:
+                cur[z, PAD - 1:PAD, :] = gx_buf[n, 0, z:z + 1]
+                cur[z, PAD + CX:PAD + CX + 1, :] = gx_buf[n, 1, z:z + 1]
         both = jnp.concatenate(
-            [gy_buf[k, 0], gy_buf[k, 1], jnp.zeros((112, CX), F32)], axis=0
+            [gy_buf[n, 0], gy_buf[n, 1], jnp.zeros((112, CX), F32)], axis=0
         )
-        hy[...] = jnp.transpose(both)
+        hy[part] = jnp.transpose(both)
 
     def inner_planes(cur, old, dst, dst_pad, source, ahead=None):
         def inner(i, carry):
             for z in (2 * i + 1, 2 * i + 2):
                 plane(
-                    cur, old, dst, dst_pad, z,
+                    0, cur, old, dst, dst_pad, z,
                     lambda rows, flat, cols: cur[z - 1, rows, cols],
                     lambda rows, flat, cols: cur[z + 1, rows, cols],
                     source,
@@ -346,6 +359,28 @@
 
         lax.fori_loop(0, CZ // 2 - 1, inner, 0)
 
+    def add_strips(k, cur, dst, dst_pad):
+        ghosts_xy(k, 0, cur)
+
+        def one(z, carry):
+            for r0 in range(0, CX, ROWS):
+                rows = pl.ds(dst_pad + r0, ROWS)
+                flat = pl.ds(r0, ROWS)
+                h = hy[0, flat, :]
+                left = jnp.where(first, pltpu.roll(h, lax.rem(128 - z, 128), 1), 0.0)
+                right = jnp.where(last, pltpu.roll(h, 119 - z, 1), 0.0)
+                dst[z, rows, 0:128] = dst[z, rows, 0:128] + q[z, flat, 0:128] * left
+                dst[z, rows, 128:256] = dst[z, rows, 128:256] + q[z, flat, 128:256] * right
+            return carry
+
+        lax.fori_loop(1, CZ - 1, one, 0)
+        for z in range(1, CZ - 1):
+            for side, row in ((0, 0), (1, CX - 1)):
+                at_row = pl.ds(dst_pad + row, 1)
+                dst[z, at_row, :] = (
+                    dst[z, at_row, :] + q[z, row:row + 1, :] * gx_buf[2 * k, side, z:z + 1, :]
+                )
+
     def end_plane(k, side, cur, old, dst, dst_pad, source):
         def ghost(rows, flat, cols):
             if k == 0:
@@ -355,14 +390,15 @@
             return (code.reshape(ROWS // 8, 8, 128) * scale[None]).reshape(ROWS, 128)
 
         plane(
-            cur, old, dst, dst_pad, side * (CZ - 1),
+            1, cur, old, dst, dst_pad, side * (CZ - 1),
             ghost,
             lambda rows, flat, cols: cur[1 + side * (CZ - 3), rows, cols],
             source,
         )
 
-    ghosts_xy(0, fa)
     inner_planes(fa, fb, fb, PAD, None)
+    add_strips(0, fa, fb, PAD)
+    ghosts_xy(0, 1, fa)
     wait_ghost(0, 0)
     end_plane(0, 0, fa, fb, fb, PAD, None)
     end_plane(0, 1, fa, fb, fb, PAD, None)
@@ -419,7 +455,8 @@
         return carry
 
     lax.fori_loop(0, CZ // 2 - 1, first_sources, 0)
-    pack_xy(1, fb, lambda: source_ends(1))
+    pack_xy(1, 0, fb, lambda: source_ends(1))
+    pack_xy(1, 1, fb)
 
     off_chip = lax.rem(t, 2)
     for k in range(1, STEPS):
@@ -431,21 +468,25 @@
         if final:
             copy_prev = pltpu.make_async_copy(cur.at[:, pl.ds(PAD, CX), :], outp_ref, osem.at[0])
             copy_prev.start()
-        ghosts_xy(k, cur)
         inner_planes(cur, nxt, dst, dst_pad, source, None if final else k + 1)
+        add_strips(k, cur, dst, dst_pad)
+        if not final:
+            pack_xy(k + 1, 0, nxt, lambda: source_ends(k + 1))
+        ghosts_xy(k, 1, cur)
         for side in (1 - off_chip, off_chip):
             wait_face(k, side)
             end_plane(k, side, cur, nxt, dst, dst_pad, source)
             if not final:
                 send_face(k + 1, side, nxt)
         if not final:
-            pack_xy(k + 1, nxt, lambda: source_ends(k + 1))
+            pack_xy(k + 1, 1, nxt)
 
     all_rows.wait_send()
     wait_sent(0, 0)
     for k in range(STEPS):
-        wait_sent(1, k)
-        wait_sent(2, k)
+        for n in (2 * k, 2 * k + 1):
+            wait_sent(1, n)
+            wait_sent(2, n)
         if k:
             wait_faces_sent(k)
     copy_prev.wait()
@@ -484,11 +525,11 @@
             pltpu.VMEM((STEPS - 1, 2, 8, CY), F32),
             pltpu.VMEM((STEPS - 1, 2, CX, CY), jnp.int16),
             pltpu.VMEM((STEPS - 1, 2, 8, CY), F32),
-            pltpu.VMEM((STEPS, 2, CZ, CY), F32),
-            pltpu.VMEM((STEPS, 2, CZ, CX), F32),
-            pltpu.VMEM((STEPS, 2, CZ, CY), F32),
-            pltpu.VMEM((STEPS, 2, CZ, CX), F32),
-            pltpu.VMEM((CX, 128), F32),
+            pltpu.VMEM((2 * STEPS, 2, CZ, CY), F32),
+            pltpu.VMEM((2 * STEPS, 2, CZ, CX), F32),
+            pltpu.VMEM((2 * STEPS, 2, CZ, CY), F32),
+            pltpu.VMEM((2 * STEPS, 2, CZ, CX), F32),
+            pltpu.VMEM((2, CX, 128), F32),
             pltpu.VMEM((CZ * CX, CAP * 128), BF16),
             pltpu.VMEM((STEPS, CAP * 128, CY), BF16),
             pltpu.VMEM((STEPS, CAP * 128, CY), BF16),
@@ -501,10 +542,10 @@
             dma((STEPS, 2)),
             dma((STEPS, 2)),
             dma((STEPS, 2)),
-            dma((STEPS, 2)),
-            dma((STEPS, 2)),
-            dma((STEPS, 2)),
-            dma((STEPS, 2)),
+            dma((2 * STEPS, 2)),
+            dma((2 * STEPS, 2)),
+            dma((2 * STEPS, 2)),
+            dma((2 * STEPS, 2)),
             dma((1,)),
             dma((1,)),
         ],

time: 43.7 us -> 42.8 us (0.979)
  Pallas kernels: 43 us -> 42 us
    pallas_call x1, Pallas kernels: 40.9 us -> 40 us  [body(): pl.pallas_call(kernel, out_shape=(pltpu.VMEM((CZ, CX, CY), F32), pltpu.VM...]
where the time goes in v4:
time: 42.8 us; the launch traced here: 42.7 us
  Pallas kernels  42 us (98%)
  between operations  0.64 us (1%)
    pallas_call x1, Pallas kernels, body(): pl.pallas_call(kernel, out_shape=(pltpu.VMEM((CZ, CX, CY), F32), pltpu.VM...  40 us
    pallas_call x1, Pallas kernels, body(): pl.pallas_call(put_out, out_shape=(field, field), in_specs=[vmem] * 2, ou...  2.03 us

profile of v4, /device:TPU:1, one launch (start us, length us, event | category | flops | bytes accessed | tf_op | source)
XLA Modules:
  0.0 42.7 jit_solution(2931855990549724583)
XLA Ops:
  0.6 40.0 %shard_map.104 = (f32[8,256,256]{2,1,0:T(8,128)S(1)}, f32[8,256,256]{2,1,0:T(8,128)S(1)}) custom-call(bf16[256,4,256]{2,1,0:T(4,128)(2,1)} %traces_hbm.1, bf16[4,256]{1,0:T(4,128)(2,1)} %bitcast.4, f32[256,256]{1,0:T(8,128)} %constant.2.clone.win_ref, s32[1,256]{1,0:T(1,128)} %bitcast.5, s32[1,256]{1,0:T(1,128)} %bitcast.6, s32[1,256]{1,0:T(1,128)} %bitcast.7, ...), custom_call_target="tpu_custom_call" | custom-call | tf_op jit(solution)/shard_map/pallas_call | solution.py:511
  40.6 2.0 %shard_map.105 = (f32[8,256,256]{2,1,0:T(8,128)}, f32[8,256,256]{2,1,0:T(8,128)}) custom-call(f32[8,256,256]{2,1,0:T(8,128)S(1)} %get-tuple-element.4.p_ref, f32[8,256,256]{2,1,0:T(8,128)S(1)} %get-tuple-element.5.n_ref), custom_call_target="tpu_custom_call" | custom-call | tf_op jit(solution)/shard_map/pallas_call | solution.py:567

commit v5 on v4

--- a/solution.py
+++ b/solution.py
@@ -59,18 +59,28 @@
     for c in loads:
         c.start()
 
-    def peer(d):
-        k = lax.rem(me + d, n_dev)
-        return k, (k // (NGX * NGY), lax.rem(k // NGY, NGX), lax.rem(k, NGY))
+    columns = [
+        (lax.rem(gx + dx, NGX), lax.rem(gy + dy, NGY)) for dx in range(NGX) for dy in range(NGY)
+    ]
+
+    def to_all_others(act):
+        for x, y in columns[1:]:
+            act(t, x, y)
+
+        def slab(d, carry):
+            there = lax.rem(t + d, NT_AX)
+            for x, y in columns:
+                act(there, x, y)
+            return carry
+
+        lax.fori_loop(1, NT_AX, slab, 0)
 
     barrier = pltpu.get_barrier_semaphore()
 
-    def greet(d, carry):
-        _, where = peer(d)
+    def greet(*where):
         pl.semaphore_signal(barrier, inc=1, device_id=where, device_id_type=MESH)
-        return carry
-
-    lax.fori_loop(1, n_dev, greet, 0)
+
+    to_all_others(greet)
 
     sides = (("trace", t, NT_AX), ("gx", gx, NGX), ("gy", gy, NGY))
     zsides = (sides[0],) * 3 + sides[1:]
@@ -217,26 +227,24 @@
 
     pl.semaphore_wait(barrier, n_dev - 1)
 
-    def post(d, carry):
-        k, where = peer(d)
+    def post(*where):
         pltpu.make_async_remote_copy(
-            src_ref=t1.at[k],
+            src_ref=t1.at[(where[0] * NGX + where[1]) * NGY + where[2]],
             dst_ref=b4.at[me],
             send_sem=a_s.at[0],
             recv_sem=a_r.at[0],
             device_id=where,
             device_id_type=MESH,
         ).start()
-        return carry
-
-    lax.fori_loop(1, n_dev, post, 0)
+
+    to_all_others(post)
     b4[me] = t1[me]
     all_rows = pltpu.make_async_remote_copy(
         src_ref=t1.at[pl.ds(0, n_dev - 1)],
         dst_ref=b4.at[pl.ds(0, n_dev - 1)],
         send_sem=a_s.at[0],
         recv_sem=a_r.at[0],
-        device_id=peer(1)[1],
+        device_id=(t,) + columns[1],
         device_id_type=MESH,
     )
 

time: 42.8 us -> 40 us (0.935)
  Pallas kernels: 42 us -> 39.2 us
    pallas_call x1, Pallas kernels: 40 us -> 37.2 us  [body(): pl.pallas_call(kernel, out_shape=(pltpu.VMEM((CZ, CX, CY), F32), pltpu.VM...]
where the time goes in v5:
time: 40 us; the launch traced here: 39.8 us
  Pallas kernels  39.2 us (98%)
  between operations  0.64 us (2%)
    pallas_call x1, Pallas kernels, body(): pl.pallas_call(kernel, out_shape=(pltpu.VMEM((CZ, CX, CY), F32), pltpu.VM...  37.2 us
    pallas_call x1, Pallas kernels, body(): pl.pallas_call(put_out, out_shape=(field, field), in_specs=[vmem] * 2, ou...  2.03 us

profile of v5, /device:TPU:1, one launch (start us, length us, event | category | flops | bytes accessed | tf_op | source)
XLA Modules:
  0.0 39.8 jit_solution(4587845911414965350)
XLA Ops:
  0.6 37.2 %shard_map.104 = (f32[8,256,256]{2,1,0:T(8,128)S(1)}, f32[8,256,256]{2,1,0:T(8,128)S(1)}) custom-call(bf16[256,4,256]{2,1,0:T(4,128)(2,1)} %traces_hbm.1, bf16[4,256]{1,0:T(4,128)(2,1)} %bitcast.4, f32[256,256]{1,0:T(8,128)} %constant.2.clone.win_ref, s32[1,256]{1,0:T(1,128)} %bitcast.5, s32[1,256]{1,0:T(1,128)} %bitcast.6, s32[1,256]{1,0:T(1,128)} %bitcast.7, ...), custom_call_target="tpu_custom_call" | custom-call | tf_op jit(solution)/shard_map/pallas_call | solution.py:519
  37.8 2.0 %shard_map.105 = (f32[8,256,256]{2,1,0:T(8,128)}, f32[8,256,256]{2,1,0:T(8,128)}) custom-call(f32[8,256,256]{2,1,0:T(8,128)S(1)} %get-tuple-element.4.p_ref, f32[8,256,256]{2,1,0:T(8,128)S(1)} %get-tuple-element.5.n_ref), custom_call_target="tpu_custom_call" | custom-call | tf_op jit(solution)/shard_map/pallas_call | solution.py:575

commit v6 on v5

--- a/solution.py
+++ b/solution.py
@@ -312,7 +312,7 @@
             flat = pl.ds(r0, ROWS)
             if part:
                 h = hy[part, flat, :]
-                h_lo = pltpu.roll(h, lax.rem(128 - z, 128), 1)
+                h_lo = pltpu.roll(h, (128 - z) % 128, 1)
                 h_hi = pltpu.roll(h, 119 - z, 1)
             else:
                 h_lo = h_hi = 0.0
@@ -375,13 +375,14 @@
                 rows = pl.ds(dst_pad + r0, ROWS)
                 flat = pl.ds(r0, ROWS)
                 h = hy[0, flat, :]
-                left = jnp.where(first, pltpu.roll(h, lax.rem(128 - z, 128), 1), 0.0)
+                left = jnp.where(first, pltpu.roll(h, (128 - z) % 128, 1), 0.0)
                 right = jnp.where(last, pltpu.roll(h, 119 - z, 1), 0.0)
                 dst[z, rows, 0:128] = dst[z, rows, 0:128] + q[z, flat, 0:128] * left
                 dst[z, rows, 128:256] = dst[z, rows, 128:256] + q[z, flat, 128:256] * right
             return carry
 
-        lax.fori_loop(1, CZ - 1, one, 0)
+        for z in range(1, CZ - 1):
+            one(z, 0)
         for z in range(1, CZ - 1):
             for side, row in ((0, 0), (1, CX - 1)):
                 at_row = pl.ds(dst_pad + row, 1)
@@ -462,7 +463,8 @@
         s_odd[pl.ds(z, 2)] = scattered(1, r)
         return carry
 
-    lax.fori_loop(0, CZ // 2 - 1, first_sources, 0)
+    for i in range(CZ // 2 - 1):
+        first_sources(i, 0)
     pack_xy(1, 0, fb, lambda: source_ends(1))
     pack_xy(1, 1, fb)
 

time: 40 us -> 38.2 us (0.955)
  Pallas kernels: 39.2 us -> 37.4 us
    pallas_call x1, Pallas kernels: 37.2 us -> 35.4 us  [body(): pl.pallas_call(kernel, out_shape=(pltpu.VMEM((CZ, CX, CY), F32), pltpu.VM...]
where the time goes in v6:
time: 38.2 us; the launch traced here: 38 us
  Pallas kernels  37.4 us (98%)
  between operations  0.64 us (2%)
    pallas_call x1, Pallas kernels, body(): pl.pallas_call(kernel, out_shape=(pltpu.VMEM((CZ, CX, CY), F32), pltpu.VM...  35.4 us
    pallas_call x1, Pallas kernels, body(): pl.pallas_call(put_out, out_shape=(field, field), in_specs=[vmem] * 2, ou...  2.03 us

profile of v6, /device:TPU:1, one launch (start us, length us, event | category | flops | bytes accessed | tf_op | source)
XLA Modules:
  0.0 38.0 jit_solution(10538607633218798077)
XLA Ops:
  0.6 35.4 %shard_map.104 = (f32[8,256,256]{2,1,0:T(8,128)S(1)}, f32[8,256,256]{2,1,0:T(8,128)S(1)}) custom-call(bf16[256,4,256]{2,1,0:T(4,128)(2,1)} %traces_hbm.1, bf16[4,256]{1,0:T(4,128)(2,1)} %bitcast.4, f32[256,256]{1,0:T(8,128)} %constant.2.clone.win_ref, s32[1,256]{1,0:T(1,128)} %bitcast.5, s32[1,256]{1,0:T(1,128)} %bitcast.6, s32[1,256]{1,0:T(1,128)} %bitcast.7, ...), custom_call_target="tpu_custom_call" | custom-call | tf_op jit(solution)/shard_map/pallas_call | solution.py:521
  36.0 2.0 %shard_map.105 = (f32[8,256,256]{2,1,0:T(8,128)}, f32[8,256,256]{2,1,0:T(8,128)}) custom-call(f32[8,256,256]{2,1,0:T(8,128)S(1)} %get-tuple-element.4.p_ref, f32[8,256,256]{2,1,0:T(8,128)S(1)} %get-tuple-element.5.n_ref), custom_call_target="tpu_custom_call" | custom-call | tf_op jit(solution)/shard_map/pallas_call | solution.py:577
